TPU v7x, 32 devices: a whole 2x2x4 slice. The times are simulated.
32 devices in a mesh: group: 2 (over y), swap: 8 (over z, x), image: 2 (over core).
Axes of the slice: x: 2, y: 2, z: 4, core: 2. Of those that a mesh axis runs over, the one named last changes fastest.
Arguments:
- images_in: bfloat16 [16, 1536, 4096], P(('group', 'image'), 'swap'), parts along dimension 0, may hold values from -6 to 6
- kernel: bfloat16 [1536, 49], P('swap'), may hold values from -1.75 to 1.75
- conv_bias: float32 [1536], P('swap'), may hold values from -1 to 1
- norm_gain: float32 [1536], replicated, may hold values from 0.1 to 1.9
- norm_shift: float32 [1536], replicated, may hold values from -0.5 to 0.5
- fp8_weight: bfloat16 [1536, 6144], P('swap', 'image'), may hold values from -1.875 to 1.875, as said below
- block_scale: int32 [1536, 48], P('swap', 'image'), may hold values from -7 to -5
- adapter_a: bfloat16 [1536, 32], replicated, may hold values from -0.15625 to 0.15625
- adapter_b: bfloat16 [32, 6144], P(None, 'image'), may hold values from -0.25 to 0.25
- cotangent: bfloat16 [16, 4096, 6144], P('group', 'swap', 'image'), parts along dimension 0, may hold values from -0.05 to 0.05
Outputs:
- grad_a: float32 [3072, 32], P('group'), parts along dimension 0
- grad_b: float32 [64, 6144], P('group', 'image'), parts along dimension 0
There are 2 independent parts, one for each index of `group`. A program takes and returns all parts, laid end to end along the dimension named above; an argument that names none is the same for every part. Nothing has to cross between parts.
Inputs may be any that keep to these rules, and one draw needn't show every extreme that they name: `fp8_weight`: each entry is a value of the E4M3 format: a sign times 2 to an integer power times 1 + k / 8 for an integer k of 0 to 7. `block_scale`: the entry at [c, j] is the exponent of the scale of hidden units 128 * j to 128 * j + 127 of weight row c.
All inputs are finite; a program needn't handle non-finite values.
Results may differ from a plain program's by a relative error of at most 0.00055.
The roundings to bfloat16 on the way count: a program that leaves them out, or rounds other values in their place, can miss the bound.
Values may be sent and summed in bfloat16 or wider, within the bound.
A program may use at most 192 MiB of HBM per device.

v0:
```python
import jax
import jax.numpy as jnp
from jax import lax
from jax.sharding import PartitionSpec as P

KS = 7
W = 64


adapter_scale = 2.0
norm_eps = 1e-06


def power_table(scales):
    factor = jnp.zeros(scales.shape, jnp.float32)
    for exponent in range(-12, 4):
        factor = factor + jnp.where(
            scales == exponent, jnp.float32(2.0**exponent), jnp.float32(0.0)
        )
    return factor


def decode(weight, scales):
    row_count = weight.shape[0]
    groups = scales.shape[1]
    blocks = (
        weight.reshape(row_count, groups, -1).astype(jnp.float32) * power_table(scales)[:, :, None]
    )
    return blocks.reshape(row_count, -1).astype(jnp.bfloat16)


def gelu_slope(pre_act):
    cumulative = 0.5 * (1.0 + jax.scipy.special.erf(pre_act * 0.7071067811865476))
    density = jnp.exp(-0.5 * pre_act * pre_act) * 0.3989422804014327
    return cumulative + pre_act * density


def depthwise(images, kernel, conv_bias, map_width):
    batch, channels, pixels = images.shape
    maps = images.reshape(batch, channels, pixels // map_width, map_width)
    taps = kernel.reshape(channels, 1, KS, KS)
    half_span = KS // 2
    summed = lax.conv_general_dilated(
        maps,
        taps,
        (1, 1),
        ((half_span, half_span), (half_span, half_span)),
        dimension_numbers=("NCHW", "OIHW", "NCHW"),
        feature_group_count=channels,
        preferred_element_type=jnp.float32,
    )
    summed = summed.reshape(batch, channels, pixels)
    return summed + conv_bias[None, :, None]


def shards(
    images_in,
    kernel,
    conv_bias,
    norm_gain,
    norm_shift,
    fp8_weight,
    block_scale,
    adapter_a,
    adapter_b,
    cotangent,
):
    conv = depthwise(images_in, kernel, conv_bias, W).astype(jnp.bfloat16)
    values = lax.all_to_all(conv, "swap", split_axis=2, concat_axis=1, tiled=True).astype(
        jnp.float32
    )
    average = jnp.mean(values, axis=1, keepdims=True)
    centred = values - average
    variance = jnp.mean(centred * centred, axis=1, keepdims=True)
    scaled = (
        centred * lax.rsqrt(variance + norm_eps) * norm_gain[None, :, None]
        + norm_shift[None, :, None]
    )
    normed = jnp.swapaxes(scaled, 1, 2).astype(jnp.bfloat16)
    own_rows = normed.reshape(-1, normed.shape[2])
    tokens = lax.all_gather(own_rows, "image", axis=0, tiled=True)
    zero_start = jnp.zeros((tokens.shape[0], fp8_weight.shape[1]), jnp.float32)
    local_weight = decode(fp8_weight, block_scale)
    shard_rows = lax.all_gather(local_weight, "swap", axis=0, tiled=True)
    columns = lax.slice_in_dim(tokens, 0, shard_rows.shape[0], axis=1)
    frozen = zero_start + jnp.dot(columns, shard_rows, preferred_element_type=jnp.float32)
    low_rank = jnp.dot(tokens, adapter_a, preferred_element_type=jnp.float32).astype(jnp.bfloat16)
    pre_act = frozen + adapter_scale * jnp.dot(
        low_rank, adapter_b, preferred_element_type=jnp.float32
    )
    upstream = cotangent.reshape(-1, cotangent.shape[2])
    grad_pre = (upstream.astype(jnp.float32) * gelu_slope(pre_act)).astype(jnp.bfloat16)
    grad_b_local = adapter_scale * jnp.dot(low_rank.T, grad_pre, preferred_element_type=jnp.float32)
    partial_back = jnp.dot(grad_pre, adapter_b.T, preferred_element_type=jnp.float32)
    contract = (((0,), (0,)), ((), ()))
    tokens_wide = tokens.astype(jnp.float32)
    summed_back = lax.psum(partial_back, "image")
    grad_a_local = adapter_scale * lax.dot_general(
        tokens_wide,
        summed_back,
        contract,
        precision=lax.Precision.HIGHEST,
        preferred_element_type=jnp.float32,
    )
    grad_a, grad_b = lax.psum((grad_a_local, grad_b_local), "swap")
    return (grad_a, grad_b)


def solution(mesh):
    placed = (
        P(("group", "image"), "swap", None),
        P("swap", None),
        P("swap"),
        P(),
        P(),
        P("swap", "image"),
        P("swap", "image"),
        P(),
        P(None, "image"),
        P("group", "swap", "image"),
    )
    return jax.shard_map(
        shards,
        mesh=mesh,
        in_specs=placed,
        out_specs=(P("group", None), P("group", "image")),
        check_vma=False,
    )
```

profile of v0, /device:TPU:0, one launch (start us, length us, event | category | flops | bytes accessed | tf_op | source)
XLA Modules:
  0.0 837.5 jit_solution(14557225846373415734)
XLA Ops:
  7.2 0.0 copy-start
  7.2 0.0 all-gather.3.cloned.1.call-start
  7.2 0.8 reshape.62
  8.1 10.6 %copy.43 = bf16[4,192,4096]{1,2,0:T(8,128)(2,1)} copy(bf16[4,192,4096]{2,1,0:T(8,128)(2,1)} %param.10) | data formatting | bytes 12582912 | tf_op args[0]
  18.7 11.5 %copy.54 = bf16[192,64,4,64]{0,1,3,2:T(8,128)(2,1)} copy(bf16[192,64,4,64]{0,3,1,2:T(8,128)(2,1)} %bitcast.75) | data formatting | bytes 12582912
  30.2 10.0 %pad.clone = bf16[192,64,4,72]{0,1,3,2:T(8,128)(2,1)} pad(bf16[192,64,4,64]{0,1,3,2:T(8,128)(2,1)} %copy.54, bf16[]{:T(256)} %constant.37), padding=0_0x0_0x0_0x3_5 | pad | bytes 13369346 | tf_op jit(solution)/shard_map/reshape | solution.py:40
  40.2 0.0 copy-start.2
  40.2 3.4 slice.2
  43.7 1.9 copy-done.2
  45.5 0.0 copy-start.9
  45.5 4.2 fusion.8
  49.7 0.0 copy-done.9
  49.7 95.9 %broadcast_select_fusion = f32[64,32,9,192]{3,1,2,0:T(8,128)S(1)} fusion(pred[32,9]{0,1:T(8,128)(4,1)S(1)} %copy-done.9, bf16[192,1,7,7]{0,1,3,2:T(2,128)(2,1)S(1)} %reshape.62, bf16[192,64,4,8,15]{0,1,4,3,2:T(8,128)(2,1)S(1)} %fusion.8), kind=kOutput, calls=%fused_computation.23 | convolution fusion | flops 341065728 | bytes 25971360 | tf_op jit(solution)/shard_map/conv_general_dilated | solution.py:43
  145.6 20.1 %copy.47 = f32[64,32,9,192]{3,0,2,1:T(8,128)S(1)} copy(f32[64,32,9,192]{3,1,2,0:T(8,128)S(1)} %broadcast_select_fusion) | data formatting | bytes 28311552 | tf_op jit(solution)/shard_map/conv_general_dilated | solution.py:43
  165.7 2.0 slice_bitcast_fusion
  167.7 0.0 copy-start.8
  167.8 17.9 %copy.48 = f32[4,192,64,64]{1,3,2,0:T(8,128)S(1)} copy(f32[4,192,64,64]{1,2,3,0:T(8,128)S(1)} %slice_bitcast_fusion) | data formatting | bytes 25165824 | tf_op jit(solution)/shard_map/conv_general_dilated | solution.py:43
  185.7 0.0 copy-done.8
  185.7 2.5 fusion.7
  188.3 31.9 %copy.49 = bf16[4,192,4096]{1,0,2:T(4,128)(2,1)S(1)} copy(bf16[4,192,4096]{1,2,0:T(8,128)(2,1)S(1)} %fusion.7) | data formatting | bytes 12582912 | tf_op jit(solution)/shard_map/convert_element_type | solution.py:68
  220.1 190.2 %all_to_all.4 = bf16[4,192,4096]{1,0,2:T(4,128)(2,1)} all-to-all(bf16[4,192,4096]{1,0,2:T(4,128)(2,1)S(1)} %copy.49), channel_id=1, replica_groups=mesh['group'=2,'swap'=8,'image'=2] {'swap'}, dimensions={2} | all-to-all | bytes 12582912 | tf_op jit(solution)/shard_map/all_to_all | solution.py:69
  410.4 13.5 %copy.50 = bf16[4,192,4096]{2,1,0:T(8,128)(2,1)} copy(bf16[4,192,4096]{1,0,2:T(4,128)(2,1)} %all_to_all.4) | data formatting | bytes 12582912 | tf_op jit(solution)/shard_map/all_to_all | solution.py:69
  423.9 9.1 %copy.55 = f32[96,8,8,512]{3,2,1,0:T(8,128)S(1)} copy(bf16[96,8,8,512]{3,1,2,0:T(8,128)(2,1)} %bitcast.77) | data formatting | bytes 18874368
  433.0 0.0 copy-start.1
  433.0 1.0 fusion.19
  434.0 3.5 copy-done.1
  437.4 1.6 multiply_reduce_fusion
  439.1 10.6 %bitcast_bitcast_fusion = f32[4,8,192,512]{3,1,2,0:T(8,128)} fusion(f32[4,192,8,512]{3,2,1,0:T(8,128)} %bitcast.71), kind=kLoop, calls=%fused_computation.16 | loop fusion | bytes 25165824 | tf_op jit(solution)/shard_map/convert_element_type | solution.py:69
  449.7 0.0 copy-start.6
  449.7 0.0 copy-start.7
  449.7 16.6 %copy.51 = f32[4,8,192,512]{3,2,1,0:T(8,128)} copy(f32[4,8,192,512]{3,1,2,0:T(8,128)} %bitcast_bitcast_fusion) | data formatting | bytes 25165824 | tf_op jit(solution)/shard_map/convert_element_type | solution.py:69
  466.2 0.0 copy-done.6
  466.2 0.0 copy-done.7
  466.2 0.0 copy-start.5
  466.2 0.0 copy-start.3
  466.3 9.0 %fusion.15 = bf16[4,1536,512]{2,1,0:T(8,128)(2,1)} fusion(f32[4,8,192,512]{3,2,1,0:T(8,128)} %copy.51, f32[1536]{0:T(1024)S(1)} %copy-done.6, f32[1536]{0:T(1024)S(1)} %copy-done.7, f32[4,512]{1,0:T(4,128)S(1)} %add_rsqrt_fusion, f32[4,512]{1,0:T(4,128)S(1)} %broadcast_multiply_fusion), kind=kLoop, calls=%fused_computation.21 | loop fusion | flops 15728640 | bytes 18903040 | tf_op jit(solution)/shard_map/convert_element_type | solution.py:79
  475.3 0.0 copy-start.4
  475.3 8.7 %copy.52 = bf16[4,512,1536]{2,1,0:T(8,128)(2,1)} copy(bf16[4,512,1536]{1,2,0:T(8,128)(2,1)} %bitcast.78) | data formatting | bytes 12582912 | tf_op jit(solution)/shard_map/convert_element_type | solution.py:79
  483.9 0.0 all-gather.3.cloned.1.call-update
  484.0 0.0 all-gather.5.cloned.1.call-start
  484.0 0.0 copy-done.5
  484.1 0.1 copy.53
  484.2 0.7 mul.87
  484.8 0.0 copy-done.3
  484.8 1.6 fusion.18
  486.5 0.0 all-gather.5.cloned.1.call-update
  486.5 0.0 all-reduce.4.cloned.1.call-start
  486.6 21.3 %all-gather.3.cloned.1.call-done = bf16[4096,1536]{1,0:T(8,128)(2,1)} async-done(((bf16[2048,1536]{1,0:T(8,128)(2,1)}), bf16[4096,1536]{1,0:T(8,128)(2,1)}) %all-gather.3.cloned.1.call-update) | async-done | bytes 12582928 | tf_op jit(solution)/shard_map/all_gather | solution.py:81
  507.8 0.0 copy-done.4
  507.8 8.3 convolution_convert_fusion
  516.2 0.0 copy-done
  516.2 20.3 %fusion.20 = f32[4096,3072]{1,0:T(8,128)} fusion(bf16[4096,32]{0,1:T(8,128)(2,1)S(1)} %convolution_convert_fusion, bf16[32,3072]{1,0:T(8,128)(2,1)S(1)} %copy-done), kind=kOutput, calls=%fused_computation.33 | convolution fusion | flops 805306368 | bytes 50790400 | tf_op jit(solution)/shard_map/dot_general | solution.py:88
  536.5 112.0 %all-gather.5.cloned.1.call-done = bf16[1536,3072]{1,0:T(8,128)(2,1)} async-done(((bf16[192,3072]{1,0:T(8,128)(2,1)}), bf16[1536,3072]{1,0:T(8,128)(2,1)}) %all-gather.5.cloned.1.call-update) | async-done | bytes 9437200 | tf_op jit(solution)/shard_map/all_gather | solution.py:84
  648.5 64.7 %fusion.5 = bf16[4096,3072]{1,0:T(8,128)(2,1)} fusion(bf16[4096,3072]{1,0:T(8,128)(2,1)} %bitcast.80, f32[4096,3072]{1,0:T(8,128)} %fusion.20, bf16[4096,1536]{1,0:T(8,128)(2,1)} %all-gather.3.cloned.1.call-done, bf16[1536,3072]{1,0:T(8,128)(2,1)} %all-gather.5.cloned.1.call-done), kind=kOutput, calls=%fused_computation.6 | convolution fusion | flops 38818283520 | bytes 122683392 | tf_op jit(solution)/shard_map/dot_general | solution.py:86
  713.1 12.9 %fusion.21 = f32[4096,32]{0,1:T(8,128)} fusion(bf16[4096,3072]{1,0:T(8,128)(2,1)} %fusion.5, bf16[32,3072]{1,0:T(8,128)(2,1)S(1)} %copy-done), kind=kOutput, calls=%fused_computation.34 | convolution fusion | flops 805306368 | bytes 25886720 | tf_op jit(solution)/shard_map/dot_general | solution.py:94
  726.0 0.0 all-reduce.4.cloned.1.call-update
  726.0 0.0 all-reduce.6.cloned.1.call-start
  726.1 11.7 %convolution_multiply_fusion = f32[32,3072]{1,0:T(8,128)} fusion(bf16[4096,32]{0,1:T(8,128)(2,1)S(1)} %convolution_convert_fusion, bf16[4096,3072]{1,0:T(8,128)(2,1)} %fusion.5), kind=kOutput, calls=%fused_computation.25 | convolution fusion | flops 805404672 | bytes 25821184 | tf_op jit(solution)/shard_map/dot_general | solution.py:93
  737.7 5.2 all-reduce.4.cloned.1.call-done
  743.0 9.8 %convolution_multiply_fusion.1 = f32[1536,32]{0,1:T(8,128)} fusion(bf16[4096,1536]{1,0:T(8,128)(2,1)} %all-gather.3.cloned.1.call-done, f32[4096,32]{0,1:T(8,128)} %all-reduce.4.cloned.1.call-done), kind=kOutput, calls=%fused_computation.28 | convolution fusion | flops 2415968256 | bytes 13303808 | tf_op jit(solution)/shard_map/dot_general | solution.py:98
  752.8 0.0 all-reduce.6.cloned.1.call-update
  752.8 74.7 %all-reduce.6.cloned.1.call-done = (f32[1536,32]{0,1:T(8,128)}, f32[32,3072]{1,0:T(8,128)}) async-done(((f32[1536,32]{0,1:T(8,128)}, f32[32,3072]{1,0:T(8,128)}), (f32[1536,32]{0,1:T(8,128)}, f32[32,3072]{1,0:T(8,128)})) %all-reduce.6.cloned.1.call-update) | async-done | bytes 589840 | tf_op jit(solution)/shard_map/psum | solution.py:105
  827.4 1.6 copy.67
  829.1 1.8 copy.68
  (3 shorter events, 0.1 us)
Async XLA Ops:
  7.2 509.0 %copy-start = (bf16[32,3072]{1,0:T(8,128)(2,1)S(1)}, bf16[32,3072]{1,0:T(8,128)(2,1)}, u32[]{:S(2)}) copy-start(bf16[32,3072]{1,0:T(8,128)(2,1)} %param.18) | copy-start | bytes 589828
  7.2 500.7 %all-gather.3.cloned.1.call-start = ((), (), s32[]{:S(2)}) async-start(), calls=%async_computation.1 | async-start | bytes 18874368 | tf_op jit(solution)/shard_map/all_gather | solution.py:81
  40.2 5.3 copy-start.2
  45.5 4.2 copy-start.9
  167.7 17.9 %copy-start.8 = (f32[192]{0:T(256)S(1)}, f32[192]{0:T(256)}, u32[]{:S(2)}) copy-start(f32[192]{0:T(256)} %param.12) | copy-start | bytes 2308
  433.0 4.5 copy-start.1
  449.7 16.6 %copy-start.6 = (f32[1536]{0:T(1024)S(1)}, f32[1536]{0:T(1024)}, u32[]{:S(2)}) copy-start(f32[1536]{0:T(1024)} %param.14) | copy-start | bytes 18436
  449.7 16.6 %copy-start.7 = (f32[1536]{0:T(1024)S(1)}, f32[1536]{0:T(1024)}, u32[]{:S(2)}) copy-start(f32[1536]{0:T(1024)} %param.13) | copy-start | bytes 18436
  466.2 17.8 %copy-start.5 = (s32[192,24]{0,1:T(8,128)S(1)}, s32[192,24]{0,1:T(8,128)}, u32[]{:S(2)}) copy-start(s32[192,24]{0,1:T(8,128)} %param.16) | copy-start | bytes 55300
  466.2 18.6 %copy-start.3 = (bf16[192,3072]{1,0:T(8,128)(2,1)S(1)}, bf16[192,3072]{1,0:T(8,128)(2,1)}, u32[]{:S(2)}) copy-start(bf16[192,3072]{1,0:T(8,128)(2,1)} %param.15) | copy-start | bytes 3538948
  475.3 32.6 %copy-start.4 = (bf16[1536,32]{0,1:T(8,128)(2,1)S(1)}, bf16[1536,32]{0,1:T(8,128)(2,1)}, u32[]{:S(2)}) copy-start(bf16[1536,32]{0,1:T(8,128)(2,1)} %param.17) | copy-start | bytes 294916
  484.0 164.5 %all-gather.5.cloned.1.call-start = ((), (), s32[]{:S(2)}) async-start(), calls=%async_computation.2 | async-start | bytes 10616832 | tf_op jit(solution)/shard_map/all_gather | solution.py:84
  486.5 256.4 %all-reduce.4.cloned.1.call-start = ((), (), s32[]{:S(2)}) async-start(), calls=%async_computation.3 | async-start | bytes 1048576 | tf_op jit(solution)/shard_map/psum | solution.py:97
  726.0 101.4 %all-reduce.6.cloned.1.call-start = ((), (), s32[]{:S(2)}) async-start(), calls=%async_computation.4 | async-start | bytes 1179648 | tf_op jit(solution)/shard_map/psum | solution.py:105
Sparse Core Ops, SparseCore 0:
  484.1 23.7 all-gather.2
  510.0 138.3 all-gather.4
  726.1 16.7 all-reduce.3
  752.9 74.4 all-reduce.5
where the time goes:
time: 845 us; the launch traced here: 838 us
  matrix products  223 us (26%)
  waiting for transfers between devices  213 us (25%)
  blocking collectives  190 us (22%)
  local copies, waits for them, and re-layouts  176 us (21%)
  other arithmetic  20 us (2%)
  between operations  14.1 us (2%)
    all_to_all x1, blocking collectives, shards(): lax.all_to_all(conv, 'swap', split_axis=2, concat_axis=1, tiled=True)  190 us
    all_gather x1, waiting for transfers between devices, shards(): shard_rows = lax.all_gather(local_weight, 'swap', axis=0, tiled=True)  112 us
    conv_general_dilated x1, matrix products, depthwise(): lax.conv_general_dilated(maps, taps, (1, 1), ((half_span, half_span), (ha...  95.9 us
    psum x1, waiting for transfers between devices, shards(): grad_a, grad_b = lax.psum((grad_a_local, grad_b_local), 'swap')  74.7 us
    dot_general x1, matrix products, shards(): jnp.dot(columns, shard_rows, preferred_element_type=jnp.float32)  64.7 us
    conv_general_dilated x4, local copies, waits for them, and re-layouts, depthwise(): lax.conv_general_dilated(maps, taps, (1, 1), ((half_span, half_span), (ha...  43.4 us
    unnamed x25, local copies, waits for them, and re-layouts  40 us
    convert_element_type x1, local copies, waits for them, and re-layouts, shards(): conv = depthwise(images_in, kernel, conv_bias, W).astype(jnp.bfloat16)  31.9 us
  transfers between devices with their start and end apart: 4, of which 4 were waited for; matrix products, arithmetic and copies ran while one was open for 5% of the time, Pallas kernels for 0%

commit v1 on v0

--- a/solution.py
+++ b/solution.py
@@ -1,10 +1,19 @@
+import functools
+
 import jax
 import jax.numpy as jnp
 from jax import lax
+from jax.experimental import pallas as pl
+from jax.experimental.pallas import tpu as pltpu
 from jax.sharding import PartitionSpec as P
 
 KS = 7
 W = 64
+HALF = KS // 2
+MESH = pl.DeviceIdType.MESH
+CH = 16
+SPAN = 1024
+MARGIN = 256
 
 
 adapter_scale = 2.0
@@ -30,9 +39,428 @@
 
 
 def gelu_slope(pre_act):
-    cumulative = 0.5 * (1.0 + jax.scipy.special.erf(pre_act * 0.7071067811865476))
+    cumulative = 0.5 * (1.0 + lax.erf(pre_act * 0.7071067811865476))
     density = jnp.exp(-0.5 * pre_act * pre_act) * 0.3989422804014327
     return cumulative + pre_act * density
+
+
+def conv_block(x_ref, k_ref, b_ref, block, shifted, taps, put):
+    pixels = x_ref.shape[-1]
+    rows = pl.ds(pl.multiple_of(block * CH, CH), CH)
+    x = x_ref[rows, :].astype(jnp.float32)
+    column = lax.broadcasted_iota(jnp.int32, (CH, pixels), 1) & (W - 1)
+    for b in range(KS):
+        step = b - HALF
+        if step == 0:
+            moved = x
+        else:
+            moved = pltpu.roll(x, (-step) % pixels, axis=1)
+            inside = column + step
+            moved = jnp.where((inside >= 0) & (inside < W), moved, 0.0)
+        shifted[b, :, MARGIN : MARGIN + pixels] = moved
+    k = k_ref[rows, :].astype(jnp.float32)
+    for t in range(KS * KS):
+        taps[t] = jnp.broadcast_to(k[:, t : t + 1], (CH, 128))
+    bias = b_ref[rows, :]
+
+    def part(i, carry):
+        start = i * SPAN
+        even = jnp.broadcast_to(bias, (CH, SPAN))
+        odd = jnp.zeros((CH, SPAN + 128), jnp.float32)
+        for a in range(KS):
+            step = a - HALF
+            for b in range(KS):
+                tap = taps[a * KS + b]
+                if step % 2 == 0:
+                    at = pl.ds(pl.multiple_of(start + MARGIN + step * W, 128), SPAN)
+                    even = even + shifted[b, :, at] * jnp.tile(tap, (1, SPAN // 128))
+                else:
+                    at = pl.ds(pl.multiple_of(start + MARGIN + (step - 1) * W, 128), SPAN + 128)
+                    odd = odd + shifted[b, :, at] * jnp.tile(tap, (1, SPAN // 128 + 1))
+        moved = pltpu.roll(odd, SPAN + 128 - W, axis=1)[:, :SPAN]
+        put(i, (even + moved).astype(jnp.bfloat16))
+        return carry
+
+    lax.fori_loop(0, pixels // SPAN, part, 0)
+
+
+def exchange_kernel(
+    n,
+    x_hbm,
+    k_ref,
+    b_ref,
+    out_hbm,
+    x_buf,
+    shifted,
+    taps,
+    stage,
+    load_sem,
+    own_sem,
+    send_sem,
+    recv_sem,
+    fsend_sem,
+    frecv_sem,
+):
+    images, channels, pixels = x_hbm.shape
+    piece = pixels // n
+    me = lax.axis_index("swap")
+    core = lax.axis_index("image")
+    other = 1 - core
+    first = core * images
+    for i in range(images):
+        pltpu.make_async_copy(x_hbm.at[i], x_buf.at[i], load_sem.at[i]).start()
+    barrier = pltpu.get_barrier_semaphore()
+    for k in range(1, n):
+        pl.semaphore_signal(
+            barrier, inc=1, device_id={"swap": lax.rem(me + k, n)}, device_id_type=MESH
+        )
+    pl.semaphore_signal(barrier, inc=1, device_id={"image": other}, device_id_type=MESH)
+    shifted[...] = jnp.zeros_like(shifted)
+    pl.semaphore_wait(barrier, n)
+
+    my_rows = pl.ds(pl.multiple_of(me * channels, channels), channels)
+
+    def sent(i, k):
+        peer = lax.rem(me + k, n)
+        return pltpu.make_async_remote_copy(
+            src_ref=stage.at[i, peer],
+            dst_ref=out_hbm.at[first + i, my_rows],
+            send_sem=send_sem.at[i, k],
+            recv_sem=recv_sem.at[i, k],
+            device_id={"swap": peer},
+            device_id_type=MESH,
+        )
+
+    def own(i):
+        return pltpu.make_async_copy(
+            stage.at[i, me], out_hbm.at[first + i, my_rows], own_sem.at[i]
+        )
+
+    def forward(i):
+        return pltpu.make_async_remote_copy(
+            src_ref=out_hbm.at[first + i],
+            dst_ref=out_hbm.at[first + i],
+            send_sem=fsend_sem.at[i],
+            recv_sem=frecv_sem.at[i],
+            device_id={"image": other},
+            device_id_type=MESH,
+        )
+
+    for i in range(images):
+        pltpu.make_async_copy(x_hbm.at[i], x_buf.at[i], load_sem.at[i]).wait()
+
+        def one(block, carry):
+            rows = pl.ds(pl.multiple_of(block * CH, CH), CH)
+
+            def put(j, values):
+                for s in range(SPAN // piece):
+                    stage[i, j * (SPAN // piece) + s, rows, :] = values[
+                        :, s * piece : (s + 1) * piece
+                    ]
+
+            conv_block(x_buf.at[i], k_ref, b_ref, block, shifted, taps, put)
+            return carry
+
+        lax.fori_loop(0, channels // CH, one, 0)
+        for k in range(1, n):
+            sent(i, k).start()
+        own(i).start()
+    for i in range(images):
+        for k in range(1, n):
+            sent(i, k).wait_recv()
+        own(i).wait()
+        forward(i).start()
+    for i in range(images):
+        forward(i).wait_recv()
+    for i in range(images):
+        for k in range(1, n):
+            sent(i, k).wait_send()
+        forward(i).wait_send()
+
+
+def exchange(n, images_in, kernel, conv_bias):
+    images, channels, pixels = images_in.shape
+    piece = pixels // n
+    dma = pltpu.SemaphoreType.DMA
+    return pl.pallas_call(
+        functools.partial(exchange_kernel, n),
+        out_shape=jax.ShapeDtypeStruct((2 * images, channels * n, piece), jnp.bfloat16),
+        in_specs=[
+            pl.BlockSpec(memory_space=pltpu.HBM),
+            pl.BlockSpec(memory_space=pltpu.VMEM),
+            pl.BlockSpec(memory_space=pltpu.VMEM),
+        ],
+        out_specs=pl.BlockSpec(memory_space=pltpu.HBM),
+        scratch_shapes=[
+            pltpu.VMEM((images, channels, pixels), jnp.bfloat16),
+            pltpu.VMEM((KS, CH, pixels + 2 * MARGIN), jnp.float32),
+            pltpu.VMEM((KS * KS, CH, 128), jnp.float32),
+            pltpu.VMEM((images, n, channels, piece), jnp.bfloat16),
+            dma((images,)),
+            dma((images,)),
+            dma((images, n)),
+            dma((images, n)),
+            dma((images,)),
+            dma((images,)),
+        ],
+        compiler_params=pltpu.CompilerParams(
+            collective_id=0, has_side_effects=True, vmem_limit_bytes=48 * 2**20
+        ),
+        cost_estimate=pl.CostEstimate(
+            flops=int(2e11), bytes_accessed=int(4e7), transcendentals=0
+        ),
+        name="conv_exchange",
+    )(images_in, kernel, conv_bias)
+
+
+def main_kernel(x_ref, w_ref, cot_ref, a_ref, b_ref, gain_ref, shift_ref, ga_ref, gb_ref, tok):
+    @pl.when(pl.program_id(0) == 0)
+    def _():
+        ga_ref[...] = jnp.zeros_like(ga_ref)
+        gb_ref[...] = jnp.zeros_like(gb_ref)
+
+    channels, piece = x_ref.shape[1:]
+    hidden = w_ref.shape[1]
+    lanes = 128
+    for s in range(piece // lanes):
+        at = slice(s * lanes, (s + 1) * lanes)
+        x = x_ref[0, :, at].astype(jnp.float32)
+        average = jnp.sum(x, axis=0, keepdims=True) * (1.0 / channels)
+        centred = x - average
+        variance = jnp.sum(centred * centred, axis=0, keepdims=True) * (1.0 / channels)
+        scaled = centred * lax.rsqrt(variance + norm_eps) * gain_ref[...] + shift_ref[...]
+        tok[at, :] = jnp.swapaxes(scaled, 0, 1).astype(jnp.bfloat16)
+    tokens = tok[...]
+    low = jnp.dot(tokens, a_ref[...], preferred_element_type=jnp.float32).astype(jnp.bfloat16)
+    low_t = jnp.swapaxes(low.astype(jnp.float32), 0, 1).astype(jnp.bfloat16)
+    step = 512
+
+    def columns(j, back):
+        at = pl.ds(pl.multiple_of(j * step, step), step)
+        up = b_ref[:, at]
+        pre = jnp.dot(tokens, w_ref[:, at], preferred_element_type=jnp.float32)
+        pre = pre + adapter_scale * jnp.dot(low, up, preferred_element_type=jnp.float32)
+        grad = (cot_ref[0, :, at].astype(jnp.float32) * gelu_slope(pre)).astype(jnp.bfloat16)
+        gb_ref[:, at] += adapter_scale * jnp.dot(low_t, grad, preferred_element_type=jnp.float32)
+        return back + lax.dot_general(
+            up, grad, (((1,), (1,)), ((), ())), preferred_element_type=jnp.float32
+        )
+
+    back = jnp.zeros((b_ref.shape[0], piece), jnp.float32)
+    for j in range(hidden // step):
+        back = columns(j, back)
+    high = back.astype(jnp.bfloat16)
+    rest = back - high.astype(jnp.float32)
+    middle = rest.astype(jnp.bfloat16)
+    least = (rest - middle.astype(jnp.float32)).astype(jnp.bfloat16)
+    total = jnp.dot(high, tokens, preferred_element_type=jnp.float32)
+    total = total + jnp.dot(middle, tokens, preferred_element_type=jnp.float32)
+    total = total + jnp.dot(least, tokens, preferred_element_type=jnp.float32)
+    ga_ref[...] += adapter_scale * total
+
+
+def main_part(conv, weight, cotangent, adapter_a, adapter_b, gain, shift):
+    images, channels, piece = conv.shape
+    hidden = weight.shape[1]
+    rank = adapter_a.shape[1]
+    once = lambda shape: pl.BlockSpec(
+        shape, lambda i: (0,) * len(shape), pipeline_mode=pl.Buffered(1)
+    )
+    return pl.pallas_call(
+        main_kernel,
+        grid=(images,),
+        out_shape=(
+            jax.ShapeDtypeStruct((rank, channels), jnp.float32),
+            jax.ShapeDtypeStruct((rank, hidden), jnp.float32),
+        ),
+        in_specs=[
+            pl.BlockSpec((1, channels, piece), lambda i: (i, 0, 0)),
+            once((channels, hidden)),
+            pl.BlockSpec((1, piece, hidden), lambda i: (i, 0, 0)),
+            once((channels, rank)),
+            once((rank, hidden)),
+            once((channels, 1)),
+            once((channels, 1)),
+        ],
+        out_specs=(
+            pl.BlockSpec((rank, channels), lambda i: (0, 0)),
+            pl.BlockSpec((rank, hidden), lambda i: (0, 0)),
+        ),
+        scratch_shapes=[pltpu.VMEM((piece, channels), jnp.bfloat16)],
+        compiler_params=pltpu.CompilerParams(
+            dimension_semantics=("arbitrary",), vmem_limit_bytes=56 * 2**20
+        ),
+        cost_estimate=pl.CostEstimate(
+            flops=int(4.4e10), bytes_accessed=int(5e7), transcendentals=int(2.5e7)
+        ),
+        name="tokens_main",
+    )(conv, weight, cotangent, adapter_a, adapter_b, gain[:, None], shift[:, None])
+
+
+def sum_kernel(n, ga_ref, gb_ref, oa_ref, ob_ref, pair, held, parts, total, pair_sem, s1, r1, s2, r2):
+    me = lax.axis_index("swap")
+    other = 1 - lax.axis_index("image")
+    rank, wide_a = ga_ref.shape
+    wide_b = gb_ref.shape[1]
+    per = n // (rank // 8)
+    ca, cb = wide_a // per, wide_b // per
+    barrier = pltpu.get_barrier_semaphore()
+    for k in range(1, n):
+        pl.semaphore_signal(
+            barrier, inc=1, device_id={"swap": lax.rem(me + k, n)}, device_id_type=MESH
+        )
+    pl.semaphore_signal(barrier, inc=1, device_id={"image": other}, device_id_type=MESH)
+    pl.semaphore_wait(barrier, n)
+    swap_a = pltpu.make_async_remote_copy(
+        src_ref=ga_ref,
+        dst_ref=pair,
+        send_sem=pair_sem.at[0],
+        recv_sem=pair_sem.at[1],
+        device_id={"image": other},
+        device_id_type=MESH,
+    )
+    swap_a.start()
+
+    def place(ref, j, width):
+        return ref.at[
+            pl.ds(pl.multiple_of((j // per) * 8, 8), 8),
+            pl.ds(pl.multiple_of((j % per) * width, 128), width),
+        ]
+
+    def move(src, dst, peer, ss, rs):
+        return pltpu.make_async_remote_copy(
+            src_ref=src,
+            dst_ref=dst,
+            send_sem=ss,
+            recv_sem=rs,
+            device_id={"swap": peer},
+            device_id_type=MESH,
+        )
+
+    def scatter_b(k):
+        peer = lax.rem(me + k, n)
+        return move(
+            place(gb_ref, peer, cb), parts.at[k, :, ca : ca + cb], peer, s1.at[1, k], r1.at[1, k]
+        )
+
+    def scatter_a(k):
+        peer = lax.rem(me + k, n)
+        return move(
+            place(held, peer, ca), parts.at[k, :, 0:ca], peer, s1.at[0, k], r1.at[0, k]
+        )
+
+    for k in range(1, n):
+        scatter_b(k).start()
+    swap_a.wait()
+    held[...] = ga_ref[...] + pair[...]
+    for k in range(1, n):
+        scatter_a(k).start()
+    sum_b = place(gb_ref, me, cb)[...]
+    for k in range(1, n):
+        scatter_b(k).wait_recv()
+        sum_b = sum_b + parts[k, :, ca : ca + cb]
+    sum_a = place(held, me, ca)[...]
+    for k in range(1, n):
+        scatter_a(k).wait_recv()
+        sum_a = sum_a + parts[k, :, 0:ca]
+    total[:, 0:ca] = sum_a
+    total[:, ca : ca + cb] = sum_b
+    place(oa_ref, me, ca)[...] = sum_a
+    place(ob_ref, me, cb)[...] = sum_b
+
+    def gather_a(k):
+        peer = lax.rem(me + k, n)
+        return move(total.at[:, 0:ca], place(oa_ref, me, ca), peer, s2.at[0, k], r2.at[0, k])
+
+    def gather_b(k):
+        peer = lax.rem(me + k, n)
+        return move(
+            total.at[:, ca : ca + cb], place(ob_ref, me, cb), peer, s2.at[1, k], r2.at[1, k]
+        )
+
+    for k in range(1, n):
+        gather_b(k).start()
+        gather_a(k).start()
+    for k in range(1, n):
+        gather_b(k).wait_recv()
+        gather_a(k).wait_recv()
+    for k in range(1, n):
+        scatter_a(k).wait_send()
+        scatter_b(k).wait_send()
+        gather_a(k).wait_send()
+        gather_b(k).wait_send()
+
+
+def sum_all(n, grad_a, grad_b):
+    rank, wide_a = grad_a.shape
+    wide_b = grad_b.shape[1]
+    per = n // (rank // 8)
+    wide = wide_a // per + wide_b // per
+    dma = pltpu.SemaphoreType.DMA
+    vmem = pl.BlockSpec(memory_space=pltpu.VMEM)
+    return pl.pallas_call(
+        functools.partial(sum_kernel, n),
+        out_shape=(
+            jax.ShapeDtypeStruct(grad_a.shape, jnp.float32),
+            jax.ShapeDtypeStruct(grad_b.shape, jnp.float32),
+        ),
+        in_specs=[vmem, vmem],
+        out_specs=(vmem, vmem),
+        scratch_shapes=[
+            pltpu.VMEM(grad_a.shape, jnp.float32),
+            pltpu.VMEM(grad_a.shape, jnp.float32),
+            pltpu.VMEM((n, 8, wide), jnp.float32),
+            pltpu.VMEM((8, wide), jnp.float32),
+            dma((2,)),
+            dma((2, n)),
+            dma((2, n)),
+            dma((2, n)),
+            dma((2, n)),
+        ],
+        compiler_params=pltpu.CompilerParams(collective_id=1, has_side_effects=True),
+        name="sum_grads",
+    )(grad_a, grad_b)
+
+
+def fast_shards(
+    n,
+    images_in,
+    kernel,
+    conv_bias,
+    norm_gain,
+    norm_shift,
+    fp8_weight,
+    block_scale,
+    adapter_a,
+    adapter_b,
+    cotangent,
+):
+    weight = lax.all_gather(decode(fp8_weight, block_scale), "swap", axis=0, tiled=True)
+    conv = exchange(n, images_in, kernel, conv_bias[:, None])
+    grad_a, grad_b = main_part(
+        conv, weight, cotangent, adapter_a, adapter_b, norm_gain, norm_shift
+    )
+    grad_a, grad_b = sum_all(n, grad_a, grad_b)
+    return (grad_a.T, grad_b)
+
+
+def fits(n, images_in, fp8_weight, adapter_a):
+    channels, pixels = images_in.shape[1:]
+    rank = adapter_a.shape[1]
+    piece = pixels // n
+    per = n // (rank // 8) if rank % 8 == 0 else 0
+    wide = fp8_weight.shape[1]
+    return (
+        per > 0
+        and n % (rank // 8) == 0
+        and channels % CH == 0
+        and pixels % SPAN == 0
+        and SPAN % piece == 0
+        and piece % 128 == 0
+        and wide % 512 == 0
+        and (channels * n) % (per * 128) == 0
+        and wide % (per * 128) == 0
+    )
 
 
 def depthwise(images, kernel, conv_bias, map_width):
@@ -53,7 +481,7 @@
     return summed + conv_bias[None, :, None]
 
 
-def shards(
+def plain_shards(
     images_in,
     kernel,
     conv_bias,
@@ -119,6 +547,13 @@
         P(None, "image"),
         P("group", "swap", "image"),
     )
+    n = mesh.shape["swap"]
+
+    def shards(*arrays):
+        if mesh.shape["image"] == 2 and fits(n, arrays[0], arrays[5], arrays[7]):
+            return fast_shards(n, *arrays)
+        return plain_shards(*arrays)
+
     return jax.shard_map(
         shards,
         mesh=mesh,

time: 845 us -> 431 us (0.51)
  Pallas kernels: 0 us -> 406 us
  matrix products: 223 us -> 0 us
  waiting for transfers between devices: 213 us -> 0.04 us
  blocking collectives: 190 us -> 0 us
  local copies, waits for them, and re-layouts: 176 us -> 7.68 us
  other arithmetic: 20 us -> 2.54 us
    pallas_call x0 -> x3, Pallas kernels: none -> 406 us  [the longest x1 254 us: exchange(): pl.pallas_call(functools.partial(exchange_kernel, n), out_shape=jax.Shape...]
    all_to_all x1 -> x0, blocking collectives: 190 us -> none  [shards(): lax.all_to_all(conv, 'swap', split_axis=2, concat_axis=1, tiled=True)]
    all_gather x2 -> x1, waiting for transfers between devices: 133 us -> 0.02 us  [fast_shards(): lax.all_gather(decode(fp8_weight, block_scale), 'swap', axis=0, tiled=True)]
    dot_general x6 -> x0, matrix products: 128 us -> none  [the longest x1 64.7 us: shards(): jnp.dot(columns, shard_rows, preferred_element_type=jnp.float32)]
    conv_general_dilated x1 -> x0, matrix products: 95.9 us -> none  [depthwise(): lax.conv_general_dilated(maps, taps, (1, 1), ((half_span, half_span), (ha...]
    psum x2 -> x0, waiting for transfers between devices: 79.9 us -> none  [the longest x1 74.7 us: shards(): grad_a, grad_b = lax.psum((grad_a_local, grad_b_local), 'swap')]
    convert_element_type x4 -> x0, local copies, waits for them, and re-layouts: 67.7 us -> none  [the longest x1 31.9 us: shards(): conv = depthwise(images_in, kernel, conv_bias, W).astype(jnp.bfloat16)]
    conv_general_dilated x4 -> x0, local copies, waits for them, and re-layouts: 43.4 us -> none  [depthwise(): lax.conv_general_dilated(maps, taps, (1, 1), ((half_span, half_span), (ha...]
  transfers between devices with their start and end apart: 4 -> 1, of which waited for: 4 -> 0; matrix products, arithmetic and copies ran while one was open for 5% -> 1% of each run, Pallas kernels for 0% -> 59%
where the time goes in v1:
time: 431 us
  Pallas kernels  406 us (94%)
  between operations  14.1 us (3%)
  local copies, waits for them, and re-layouts  7.68 us (2%)
    pallas_call x1, Pallas kernels, exchange(): pl.pallas_call(functools.partial(exchange_kernel, n), out_shape=jax.Shape...  254 us
    pallas_call x1, Pallas kernels, main_part(): pl.pallas_call(main_kernel, grid=(images,), out_shape=(jax.ShapeDtypeStru...  111 us
    pallas_call x1, Pallas kernels, sum_all(): pl.pallas_call(functools.partial(sum_kernel, n), out_shape=(jax.ShapeDtyp...  41.8 us
  transfers between devices with their start and end apart: 1, of which 0 were waited for; matrix products, arithmetic and copies ran while one was open for 1% of the time, Pallas kernels for 59%

profile of v1, /device:TPU:0, one launch (start us, length us, event | category | flops | bytes accessed | tf_op | source)
XLA Modules:
  0.0 430.7 jit_solution(13343177630390874518)
XLA Ops:
  7.2 0.0 copy-start
  7.2 0.0 all-gather.2.cloned.1.call-start
  7.2 0.9 select_add_fusion
  8.1 0.1 copy.17
  8.2 0.7 mul.11
  8.9 0.0 copy-done
  8.9 0.0 copy-start.2
  8.9 0.0 copy-start.5
  8.9 0.0 copy-start.1
  8.9 0.0 copy-start.3
  8.9 1.7 fusion
  10.6 0.0 copy-start.4
  10.6 0.0 all-gather.2.cloned.1.call-update
  10.6 0.0 copy-done.2
  10.6 0.1 copy.15.k_ref
  10.8 0.0 copy-done.5
  10.8 0.1 copy.16.b_ref
  10.9 0.0 copy-done.1
  10.9 0.9 copy.18.a_ref
  11.8 0.0 copy-done.3
  11.8 1.2 broadcast_in_dim.98.gain_ref
  13.0 0.0 copy-done.4
  13.0 1.2 broadcast_in_dim.99.shift_ref
  14.2 253.6 %conv_exchange.1.x_ref = bf16[8,1536,512]{2,1,0:T(8,128)(2,1)} custom-call(bf16[4,192,4096]{2,1,0:T(8,128)(2,1)} %x_hbm.1, bf16[192,49]{1,0:T(8,128)(2,1)S(1)} %copy.15.k_ref, f32[192,1]{1,0:T(8,128)S(1)} %copy.16.b_ref), custom_call_target="tpu_custom_call" | custom-call | flops 199999995904 | bytes 40000000 | tf_op jit(solution)/shard_map/conv_exchange/pallas_call | solution.py:185
  267.7 0.0 all-gather.2.cloned.1.call-done.w_ref
  267.8 110.9 %tokens_main.1 = (f32[32,1536]{1,0:T(8,128)}, f32[32,3072]{1,0:T(8,128)}) custom-call(bf16[8,1536,512]{2,1,0:T(8,128)(2,1)} %conv_exchange.1.x_ref, bf16[1536,3072]{1,0:T(8,128)(2,1)} %all-gather.2.cloned.1.call-done.w_ref, bf16[8,512,3072]{2,1,0:T(8,128)(2,1)} %cot_ref.1, bf16[1536,32]{1,0:T(8,128)(2,1)} %copy.18.a_ref, bf16[32,3072]{1,0:T(8,128)(2,1)} %b_ref.1, ...), custom_call_target="tpu_custom_call" | custom-call | flops 44000002048 | bytes 50000000 | tf_op jit(solution)/shard_map/tokens_main/pallas_call | solution.py:269
  378.7 41.8 %sum_grads.1 = (f32[32,1536]{1,0:T(8,128)}, f32[32,3072]{1,0:T(8,128)}) custom-call(f32[32,1536]{1,0:T(8,128)} %get-tuple-element.6.ga_ref, f32[32,3072]{1,0:T(8,128)} %get-tuple-element.7.gb_ref), custom_call_target="tpu_custom_call" | custom-call | tf_op jit(solution)/shard_map/sum_grads/pallas_call | solution.py:401
  420.5 1.6 copy.25
  422.1 1.8 copy.26
Async XLA Ops:
  7.2 1.7 copy-start
  7.2 260.6 %all-gather.2.cloned.1.call-start = ((), (), s32[]{:S(2)}) async-start(), calls=%async_computation | async-start | bytes 10616832 | tf_op jit(solution)/shard_map/all_gather | solution.py:438
  8.9 1.8 copy-start.2
  8.9 1.9 copy-start.5
  8.9 2.0 copy-start.1
  8.9 2.9 copy-start.3
  10.6 2.4 copy-start.4
Sparse Core Ops, SparseCore 0:
  10.7 244.4 all-gather.1

commit v2 on v1

--- a/solution.py
+++ b/solution.py
@@ -89,7 +89,9 @@
     x_hbm,
     k_ref,
     b_ref,
+    w_hbm,
     out_hbm,
+    w_out,
     x_buf,
     shifted,
     taps,
@@ -100,6 +102,11 @@
     recv_sem,
     fsend_sem,
     frecv_sem,
+    w_own_sem,
+    chain_send,
+    chain_recv,
+    side_send,
+    side_recv,
 ):
     images, channels, pixels = x_hbm.shape
     piece = pixels // n
@@ -146,6 +153,80 @@
             device_id_type=MESH,
         )
 
+    depth = w_hbm.shape[0]
+    line = n // 2
+    spot = me // 2
+    beside = me + 1 - 2 * lax.rem(me, 2)
+
+    def w_rows(block):
+        return w_out.at[pl.ds(pl.multiple_of(block * depth, depth), depth)]
+
+    def w_move(src, block, peer, ss, rs):
+        return pltpu.make_async_remote_copy(
+            src_ref=src,
+            dst_ref=w_rows(block),
+            send_sem=ss,
+            recv_sem=rs,
+            device_id={"swap": peer},
+            device_id_type=MESH,
+        )
+
+    def chain(way, s):
+        block = me - way * 2 * (s - 1)
+        src = w_hbm if s == 1 else w_rows(block)
+        d = (1 - way) // 2
+        return w_move(src, block, me + way * 2, chain_send.at[d, s], chain_recv.at[d, s])
+
+    def comes(way, s):
+        d = (1 - way) // 2
+        block = me - way * 2 * s
+        return w_move(w_rows(block), block, beside, chain_send.at[d, s], chain_recv.at[d, s])
+
+    def side(way, s):
+        block = me - way * 2 * s
+        src = w_hbm if s == 0 else w_rows(block)
+        d = (1 - way) // 2
+        return w_move(src, block, beside, side_send.at[d, s], side_recv.at[d, s])
+
+    def side_comes(way, s):
+        d = (1 - way) // 2
+        block = beside - way * 2 * s
+        return w_move(w_rows(block), block, beside, side_send.at[d, s], side_recv.at[d, s])
+
+    def held(way, s):
+        place = spot - way * s
+        return (place >= 0) & (place < line)
+
+    def sends(way, s):
+        return held(way, s - 1) & held(way, -1)
+
+    def relay(s):
+        for way in (1, -1):
+
+            @pl.when(held(way, s))
+            def _():
+                comes(way, s).wait_recv()
+                side(way, s).start()
+
+            if s + 1 < line:
+
+                @pl.when(sends(way, s + 1))
+                def _():
+                    chain(way, s + 1).start()
+
+    def w_own():
+        return pltpu.make_async_copy(w_hbm, w_rows(me), w_own_sem)
+
+    for way in (1, -1):
+
+        @pl.when(sends(way, 1))
+        def _():
+            chain(way, 1).start()
+
+    side(1, 0).start()
+    w_own().start()
+    relayed = 1
+
     for i in range(images):
         pltpu.make_async_copy(x_hbm.at[i], x_buf.at[i], load_sem.at[i]).wait()
 
@@ -165,6 +246,11 @@
         for k in range(1, n):
             sent(i, k).start()
         own(i).start()
+        if i % 2 == 1 and relayed < line:
+            relay(relayed)
+            relayed += 1
+    for s in range(relayed, line):
+        relay(s)
     for i in range(images):
         for k in range(1, n):
             sent(i, k).wait_recv()
@@ -176,21 +262,42 @@
         for k in range(1, n):
             sent(i, k).wait_send()
         forward(i).wait_send()
-
-
-def exchange(n, images_in, kernel, conv_bias):
+    w_own().wait()
+    side_comes(1, 0).wait_recv()
+    side(1, 0).wait_send()
+    for s in range(1, line):
+        for way in (1, -1):
+
+            @pl.when(held(way, s))
+            def _():
+                side_comes(way, s).wait_recv()
+                side(way, s).wait_send()
+
+            @pl.when(sends(way, s))
+            def _():
+                chain(way, s).wait_send()
+
+
+def exchange(n, images_in, kernel, conv_bias, weight):
     images, channels, pixels = images_in.shape
     piece = pixels // n
     dma = pltpu.SemaphoreType.DMA
     return pl.pallas_call(
         functools.partial(exchange_kernel, n),
-        out_shape=jax.ShapeDtypeStruct((2 * images, channels * n, piece), jnp.bfloat16),
+        out_shape=(
+            jax.ShapeDtypeStruct((2 * images, channels * n, piece), jnp.bfloat16),
+            jax.ShapeDtypeStruct((weight.shape[0] * n, weight.shape[1]), jnp.bfloat16),
+        ),
         in_specs=[
             pl.BlockSpec(memory_space=pltpu.HBM),
             pl.BlockSpec(memory_space=pltpu.VMEM),
             pl.BlockSpec(memory_space=pltpu.VMEM),
+            pl.BlockSpec(memory_space=pltpu.HBM),
         ],
-        out_specs=pl.BlockSpec(memory_space=pltpu.HBM),
+        out_specs=(
+            pl.BlockSpec(memory_space=pltpu.HBM),
+            pl.BlockSpec(memory_space=pltpu.HBM),
+        ),
         scratch_shapes=[
             pltpu.VMEM((images, channels, pixels), jnp.bfloat16),
             pltpu.VMEM((KS, CH, pixels + 2 * MARGIN), jnp.float32),
@@ -202,6 +309,11 @@
             dma((images, n)),
             dma((images,)),
             dma((images,)),
+            dma,
+            dma((2, n // 2)),
+            dma((2, n // 2)),
+            dma((2, n // 2)),
+            dma((2, n // 2)),
         ],
         compiler_params=pltpu.CompilerParams(
             collective_id=0, has_side_effects=True, vmem_limit_bytes=48 * 2**20
@@ -210,7 +322,7 @@
             flops=int(2e11), bytes_accessed=int(4e7), transcendentals=0
         ),
         name="conv_exchange",
-    )(images_in, kernel, conv_bias)
+    )(images_in, kernel, conv_bias, weight)
 
 
 def main_kernel(x_ref, w_ref, cot_ref, a_ref, b_ref, gain_ref, shift_ref, ga_ref, gb_ref, tok):
@@ -435,8 +547,9 @@
     adapter_b,
     cotangent,
 ):
-    weight = lax.all_gather(decode(fp8_weight, block_scale), "swap", axis=0, tiled=True)
-    conv = exchange(n, images_in, kernel, conv_bias[:, None])
+    conv, weight = exchange(
+        n, images_in, kernel, conv_bias[:, None], decode(fp8_weight, block_scale)
+    )
     grad_a, grad_b = main_part(
         conv, weight, cotangent, adapter_a, adapter_b, norm_gain, norm_shift
     )
@@ -452,6 +565,7 @@
     wide = fp8_weight.shape[1]
     return (
         per > 0
+        and n % 2 == 0
         and n % (rank // 8) == 0
         and channels % CH == 0
         and pixels % SPAN == 0

time: 431 us -> 381 us (0.88)
  Pallas kernels: 406 us -> 371 us
  between operations: 14.1 us -> 0.74 us
    pallas_call x1, Pallas kernels: 254 us -> 231 us  [exchange(): pl.pallas_call(functools.partial(exchange_kernel, n), out_shape=(jax.Shap...]
    pallas_call x1, Pallas kernels: 41.8 us -> 29.3 us  [sum_all(): pl.pallas_call(functools.partial(sum_kernel, n), out_shape=(jax.ShapeDtyp...]
  transfers between devices with their start and end apart: 1 -> 0, of which waited for: 0 -> 0; matrix products, arithmetic and copies ran while one was open for 1% -> 0% of each run, Pallas kernels for 59% -> 0%
where the time goes in v2:
time: 381 us
  Pallas kernels  371 us (97%)
  local copies, waits for them, and re-layouts  7.69 us (2%)
    pallas_call x1, Pallas kernels, exchange(): pl.pallas_call(functools.partial(exchange_kernel, n), out_shape=(jax.Shap...  231 us
    pallas_call x1, Pallas kernels, main_part(): pl.pallas_call(main_kernel, grid=(images,), out_shape=(jax.ShapeDtypeStru...  111 us
    pallas_call x1, Pallas kernels, sum_all(): pl.pallas_call(functools.partial(sum_kernel, n), out_shape=(jax.ShapeDtyp...  29.3 us

profile of v2, /device:TPU:0, one launch (start us, length us, event | category | flops | bytes accessed | tf_op | source)
XLA Modules:
  0.0 380.9 jit_solution(1544758480523237487)
XLA Ops:
  0.6 0.0 copy-start
  0.6 0.9 select_add_fusion
  1.5 0.1 copy.15
  1.6 0.7 mul.11
  2.3 0.0 copy-done
  2.3 0.0 copy-start.5
  2.3 0.0 copy-start.2
  2.3 0.7 fusion.w_hbm
  3.0 0.0 copy-done.5
  3.0 0.1 copy.17.b_ref
  3.1 0.0 copy-done.2
  3.1 0.1 copy.16.k_ref
  3.3 0.0 copy-start.3
  3.3 0.0 copy-start.4
  3.3 0.0 copy-start.1
  3.3 230.9 %conv_exchange.1 = (bf16[8,1536,512]{2,1,0:T(8,128)(2,1)}, bf16[1536,3072]{1,0:T(8,128)(2,1)}) custom-call(bf16[4,192,4096]{2,1,0:T(8,128)(2,1)} %x_hbm.1, bf16[192,49]{1,0:T(8,128)(2,1)S(1)} %copy.16.k_ref, f32[192,1]{1,0:T(8,128)S(1)} %copy.17.b_ref, bf16[192,3072]{1,0:T(8,128)(2,1)S(1)} %fusion.w_hbm), custom_call_target="tpu_custom_call" | custom-call | flops 199999995904 | bytes 40000000 | tf_op jit(solution)/shard_map/conv_exchange/pallas_call | solution.py:285
  234.2 0.0 copy-done.3
  234.2 1.2 broadcast_in_dim.98.gain_ref
  235.3 0.0 copy-done.4
  235.3 1.2 broadcast_in_dim.99.shift_ref
  236.5 0.0 copy-done.1
  236.5 0.9 copy.18.a_ref
  237.4 110.7 %tokens_main.1 = (f32[32,1536]{1,0:T(8,128)}, f32[32,3072]{1,0:T(8,128)}) custom-call(bf16[8,1536,512]{2,1,0:T(8,128)(2,1)} %get-tuple-element.8.x_ref, bf16[1536,3072]{1,0:T(8,128)(2,1)} %get-tuple-element.9.w_ref, bf16[8,512,3072]{2,1,0:T(8,128)(2,1)} %cot_ref.1, bf16[1536,32]{1,0:T(8,128)(2,1)} %copy.18.a_ref, bf16[32,3072]{1,0:T(8,128)(2,1)} %b_ref.1, ...), custom_call_target="tpu_custom_call" | custom-call | flops 44000002048 | bytes 50000000 | tf_op jit(solution)/shard_map/tokens_main/pallas_call | solution.py:381
  348.2 29.3 %sum_grads.1 = (f32[32,1536]{1,0:T(8,128)}, f32[32,3072]{1,0:T(8,128)}) custom-call(f32[32,1536]{1,0:T(8,128)} %get-tuple-element.10.ga_ref, f32[32,3072]{1,0:T(8,128)} %get-tuple-element.11.gb_ref), custom_call_target="tpu_custom_call" | custom-call | tf_op jit(solution)/shard_map/sum_grads/pallas_call | solution.py:513
  377.5 1.6 copy.25
  379.1 1.8 copy.26
Async XLA Ops:
  0.6 1.7 copy-start
  2.3 0.7 copy-start.5
  2.3 0.8 copy-start.2
  3.3 230.9 %copy-start.3 = (f32[1536]{0:T(1024)S(1)}, f32[1536]{0:T(1024)}, u32[]{:S(2)}) copy-start(f32[1536]{0:T(1024)} %param.13) | copy-start | bytes 18436
  3.3 232.1 %copy-start.4 = (f32[1536]{0:T(1024)S(1)}, f32[1536]{0:T(1024)}, u32[]{:S(2)}) copy-start(f32[1536]{0:T(1024)} %param.14) | copy-start | bytes 18436
  3.3 233.2 %copy-start.1 = (bf16[1536,32]{0,1:T(8,128)(2,1)S(1)}, bf16[1536,32]{0,1:T(8,128)(2,1)}, u32[]{:S(2)}) copy-start(bf16[1536,32]{0,1:T(8,128)(2,1)} %param.17) | copy-start | bytes 294916
